TPU v7x, 256 devices: a whole 4x4x8 slice. The times are simulated.
256 devices in a mesh: dp: 8 (over y, x_lo), tensor: 32 (over z, x_hi, core).
Axes of the slice: x: 4 (x_hi: 2, x_lo: 2; x = x_hi * 2 + x_lo), y: 4, z: 8, core: 2. Of those that a mesh axis runs over, the one named last changes fastest.
Arguments:
- tokens: bfloat16 [2048, 3072], P('dp', 'tensor'), may hold values from -6 to 6
- buckets: int32 [2048], P('dp'), may hold values from 0 to 999
- modulation: float32 [1000, 3, 3072], P(None, None, 'tensor'), may hold values from -3 to 3
- up_weight: bfloat16 [3072, 12288], P(None, 'tensor'), may hold values from -0.109375 to 0.109375
- down_weight: bfloat16 [3072, 12288], P(None, 'tensor'), may hold values from -0.0546875 to 0.0546875
- output_cotangent: bfloat16 [2048, 3072], P('dp', 'tensor'), may hold values from -6 to 6
Outputs:
- mixed: bfloat16 [2048, 3072], P('dp', 'tensor')
- token_input_gradient: bfloat16 [2048, 3072], P('dp', 'tensor')
- grad_up: float32 [3072, 12288], P('dp', 'tensor')
- grad_down: float32 [3072, 12288], P('dp', 'tensor')
All inputs are finite; a program needn't handle non-finite values.
Results may differ from a plain program's by a relative error of at most 0.0062.
Values may be sent and summed in bfloat16 or wider, within the bound.
A program may use at most 64 MiB of HBM per device.

v0:
```python
import jax
import jax.numpy as jnp
from jax import lax
from jax.sharding import PartitionSpec as P


def gelu_tanh(value):
    return jax.nn.gelu(value, approximate=True)


def on_device(tokens, buckets, modulation, up_weight, down_weight, output_cotangent):
    local_cols = tokens.shape[1]
    model_width = local_cols * lax.axis_size("tensor")
    input_tokens = tokens.astype(jnp.float32)
    cond = jnp.take(modulation, buckets, axis=0)
    modulation_shift = cond[:, 0]
    modulation_scale = cond[:, 1]
    gate = cond[:, 2]
    total, squares = lax.psum(
        (jnp.sum(input_tokens, axis=1), jnp.sum(input_tokens * input_tokens, axis=1)), "tensor"
    )
    row_mean = total / model_width
    var = squares / model_width - row_mean * row_mean
    inverse_deviation = lax.rsqrt(var + 1e-06)
    normalized_input = (input_tokens - row_mean[:, None]) * inverse_deviation[:, None]
    hidden_input_rows = (normalized_input * (1.0 + modulation_scale) + modulation_shift).astype(
        jnp.bfloat16
    )
    full_in = lax.all_gather(hidden_input_rows, "tensor", axis=1, tiled=True)
    pre = jnp.dot(full_in, up_weight, preferred_element_type=jnp.float32)
    act = gelu_tanh(pre).astype(jnp.bfloat16)
    block = down_weight
    velocity = lax.psum_scatter(
        lax.dot_general(block, act, (((1,), (1,)), ((), ())), preferred_element_type=jnp.float32),
        "tensor",
        scatter_dimension=0,
        tiled=True,
    ).T
    mixed = (input_tokens + gate * velocity).astype(jnp.bfloat16)
    dvel = (output_cotangent.astype(jnp.float32) * gate).astype(jnp.bfloat16)
    full_dvel = lax.all_gather(dvel, "tensor", axis=1, tiled=True)
    dact = jnp.dot(full_dvel, down_weight, preferred_element_type=jnp.float32)
    pull = jax.vjp(gelu_tanh, pre)[1]
    dpre = pull(dact)[0].astype(jnp.bfloat16)
    block = up_weight
    dh = lax.psum_scatter(
        lax.dot_general(block, dpre, (((1,), (1,)), ((), ())), preferred_element_type=jnp.float32),
        "tensor",
        scatter_dimension=0,
        tiled=True,
    ).T
    normalized_input_gradient = dh * (1.0 + modulation_scale)
    first_product, second_product = lax.psum(
        (
            jnp.sum(normalized_input_gradient, axis=1),
            jnp.sum(normalized_input_gradient * normalized_input, axis=1),
        ),
        "tensor",
    )
    token_input_gradient = output_cotangent.astype(jnp.float32) + inverse_deviation[:, None] * (
        normalized_input_gradient
        - first_product[:, None] / model_width
        - normalized_input * second_product[:, None] / model_width
    )
    cols = full_in
    grad_up = lax.psum_scatter(
        lax.dot_general(cols, dpre, (((0,), (0,)), ((), ())), preferred_element_type=jnp.float32),
        "dp",
        scatter_dimension=0,
        tiled=True,
    )
    cols = full_dvel
    grad_down = lax.psum_scatter(
        lax.dot_general(cols, act, (((0,), (0,)), ((), ())), preferred_element_type=jnp.float32),
        "dp",
        scatter_dimension=0,
        tiled=True,
    )
    return (mixed, token_input_gradient.astype(jnp.bfloat16), grad_up, grad_down)


def solution(mesh):
    placed = (
        P("dp", "tensor"),
        P("dp"),
        P(None, None, "tensor"),
        P(None, "tensor"),
        P(None, "tensor"),
        P("dp", "tensor"),
    )
    return jax.shard_map(
        on_device,
        mesh=mesh,
        in_specs=placed,
        out_specs=(P("dp", "tensor"), P("dp", "tensor"), P("dp", "tensor"), P("dp", "tensor")),
        check_vma=False,
    )
```

profile of v0, /device:TPU:1, one launch (start us, length us, event | category | flops | bytes accessed | tf_op | source)
XLA Modules:
  0.0 722.3 jit_solution(3974144515244897455)
XLA Ops:
  7.2 0.0 copy-start
  7.2 0.0 all-gather.3.cloned.1.call-start
  7.2 0.8 compare_and_fusion
  8.1 0.7 compare_select_fusion
  8.8 0.9 copy.20
  9.7 0.1 convert_reduce_fusion
  9.8 2.8 copy.21
  12.6 2.6 gather_fusion
  15.2 0.3 broadcast_select_fusion
  15.5 0.3 fusion.23
  15.8 68.9 %all-reduce.1 = (f32[256]{0:T(256)S(1)}, f32[256]{0:T(256)S(1)}) all-reduce(f32[256]{0:T(256)S(1)} %get-tuple-element.19, f32[256]{0:T(256)S(1)} %get-tuple-element.18), channel_id=1, replica_groups=mesh['dp'=8,'tensor'=32] {'tensor'}, use_global_device_ids=true, to_apply=%region_3.4 | all-reduce | flops 512 | bytes 4096 | tf_op jit(solution)/shard_map/psum | solution.py:19
  84.7 0.1 fusion.14
  84.9 0.7 copy.24
  85.6 0.0 all-gather.3.cloned.1.call-update
  85.6 0.0 reduce-scatter.13.cloned.1.call-start
  85.7 78.6 %all-gather.3.cloned.1.call-done = bf16[256,3072]{0,1:T(8,128)(2,1)} async-done(((bf16[256,96]{0,1:T(8,128)(2,1)}), bf16[256,3072]{0,1:T(8,128)(2,1)}) %all-gather.3.cloned.1.call-update) | async-done | bytes 1572880 | tf_op jit(solution)/shard_map/all_gather | solution.py:29
  164.3 3.2 fusion.24
  167.5 2.7 convolution_bitcast_fusion.1
  170.2 3.5 copy.29
  173.8 0.0 reduce-scatter.13.cloned.1.call-update
  173.8 0.0 all-gather.5.cloned.1.call-start
  173.9 0.7 copy-done.2
  174.6 0.1 copy.25
  174.7 113.5 %reduce-scatter.13.cloned.1.call-done = f32[96,256]{1,0:T(8,128)} async-done(((f32[3072,256]{1,0:T(8,128)}), f32[96,256]{1,0:T(8,128)}) %reduce-scatter.13.cloned.1.call-update) | async-done | bytes 98320
  288.2 1.0 copy.30
  289.2 0.7 copy.26
  289.9 0.0 all-gather.5.cloned.1.call-update
  290.0 0.0 reduce-scatter.15.cloned.1.call-start
  290.0 84.3 %all-gather.5.cloned.1.call-done = bf16[256,3072]{0,1:T(8,128)(2,1)} async-done(((bf16[256,96]{0,1:T(8,128)(2,1)}), bf16[256,3072]{0,1:T(8,128)(2,1)}) %all-gather.5.cloned.1.call-update) | async-done | bytes 1572880 | tf_op jit(solution)/shard_map/all_gather | solution.py:41
  374.3 2.7 fusion.6
  377.1 2.7 convolution_bitcast_fusion
  379.8 3.5 copy.31
  383.3 0.0 reduce-scatter.15.cloned.1.call-update
  383.3 0.0 reduce-scatter.11.cloned.1.call-start
  383.4 4.6 fusion.22
  388.0 0.0 reduce-scatter.11.cloned.1.call-update
  388.0 0.0 reduce-scatter.9.cloned.1.call-start
  388.1 4.6 fusion.25
  392.6 0.0 reduce-scatter.9.cloned.1.call-update
  392.6 0.7 copy.27
  393.4 104.4 %reduce-scatter.15.cloned.1.call-done = f32[96,256]{1,0:T(8,128)} async-done(((f32[3072,256]{1,0:T(8,128)}), f32[96,256]{1,0:T(8,128)}) %reduce-scatter.15.cloned.1.call-update) | async-done | bytes 98320
  497.7 1.0 copy.32
  498.7 0.2 fusion.21
  499.0 72.0 %all-reduce = (f32[256]{0:T(256)S(1)}, f32[256]{0:T(256)S(1)}) all-reduce(f32[256]{0:T(256)S(1)} %get-tuple-element.17, f32[256]{0:T(256)S(1)} %get-tuple-element.16), channel_id=1, replica_groups=mesh['dp'=8,'tensor'=32] {'tensor'}, use_global_device_ids=true, to_apply=%region_9.10 | all-reduce | flops 512 | bytes 4096 | tf_op jit(solution)/shard_map/psum | solution.py:53
  571.0 0.2 fusion.8
  571.2 0.7 copy.28
  571.9 36.7 %reduce-scatter.11.cloned.1.call-done = f32[384,384]{1,0:T(8,128)} async-done(((f32[3072,384]{1,0:T(8,128)}), f32[384,384]{1,0:T(8,128)}) %reduce-scatter.11.cloned.1.call-update) | async-done | bytes 589840 | tf_op jit(solution)/shard_map/reduce_scatter | solution.py:73
  608.7 106.7 %reduce-scatter.9.cloned.1.call-done = f32[384,384]{1,0:T(8,128)} async-done(((f32[3072,384]{1,0:T(8,128)}), f32[384,384]{1,0:T(8,128)}) %reduce-scatter.9.cloned.1.call-update) | async-done | bytes 589840 | tf_op jit(solution)/shard_map/reduce_scatter | solution.py:66
  (8 shorter events, 0.1 us)
Async XLA Ops:
  7.2 160.3 %copy-start = (bf16[3072,384]{1,0:T(8,128)(2,1)S(1)}, bf16[3072,384]{1,0:T(8,128)(2,1)}, u32[]{:S(2)}) copy-start(bf16[3072,384]{1,0:T(8,128)(2,1)} %param.10) | copy-start | bytes 7077892
  7.2 157.2 %all-gather.3.cloned.1.call-start = ((), (), s32[]{:S(2)}) async-start(), calls=%async_computation.4 | async-start | bytes 1622016 | tf_op jit(solution)/shard_map/all_gather | solution.py:29
  85.6 202.5 %reduce-scatter.13.cloned.1.call-start = ((), (), s32[]{:S(2)}) async-start(), calls=%async_computation.8 | async-start | bytes 3244032
  173.8 0.8 copy-start.2
  173.8 200.5 %all-gather.5.cloned.1.call-start = ((), (), s32[]{:S(2)}) async-start(), calls=%async_computation.5 | async-start | bytes 1622016 | tf_op jit(solution)/shard_map/all_gather | solution.py:41
  290.0 207.8 %reduce-scatter.15.cloned.1.call-start = ((), (), s32[]{:S(2)}) async-start(), calls=%async_computation.9 | async-start | bytes 3244032
  374.3 2.7 copy-start.1
  383.3 225.3 %reduce-scatter.11.cloned.1.call-start = ((), (), s32[]{:S(2)}) async-start(), calls=%async_computation.7 | async-start | bytes 5308416 | tf_op jit(solution)/shard_map/reduce_scatter | solution.py:73
  388.0 327.4 %reduce-scatter.9.cloned.1.call-start = ((), (), s32[]{:S(2)}) async-start(), calls=%async_computation.6 | async-start | bytes 5308416 | tf_op jit(solution)/shard_map/reduce_scatter | solution.py:66
Sparse Core Ops, SparseCore 0:
  85.8 78.5 all-gather.2
  173.9 114.2 reduce-scatter.12
  291.6 82.7 all-gather.4
  383.5 114.2 reduce-scatter.14
  500.7 107.9 reduce-scatter.10
  611.7 103.7 reduce-scatter.8
where the time goes:
time: 723 us; the launch traced here: 722 us
  waiting for transfers between devices  524 us (72%)
  blocking collectives  141 us (20%)
  matrix products  20.5 us (3%)
  local copies, waits for them, and re-layouts  19.3 us (3%)
  between operations  14.2 us (2%)
    unnamed x8, waiting for transfers between devices  218 us
    reduce_scatter x1, waiting for transfers between devices, on_device(): lax.psum_scatter(lax.dot_general(cols, dpre, (((0,), (0,)), ((), ())), pr...  107 us
    all_gather x1, waiting for transfers between devices, on_device(): full_dvel = lax.all_gather(dvel, 'tensor', axis=1, tiled=True)  84.3 us
    all_gather x1, waiting for transfers between devices, on_device(): full_in = lax.all_gather(hidden_input_rows, 'tensor', axis=1, tiled=True)  78.6 us
    psum x1, blocking collectives, on_device(): lax.psum((jnp.sum(normalized_input_gradient, axis=1), jnp.sum(normalized_...  72 us
    psum x1, blocking collectives, on_device(): lax.psum((jnp.sum(input_tokens, axis=1), jnp.sum(input_tokens * input_tok...  68.9 us
    reduce_scatter x1, waiting for transfers between devices, on_device(): lax.psum_scatter(lax.dot_general(cols, act, (((0,), (0,)), ((), ())), pre...  36.7 us
    unnamed x15, local copies, waits for them, and re-layouts  15 us
  transfers between devices with their start and end apart: 6, of which 6 were waited for; matrix products, arithmetic and copies ran while one was open for 2% of the time, Pallas kernels for 0%

commit v1 on v0

--- a/solution.py
+++ b/solution.py
@@ -38,7 +38,15 @@
     ).T
     mixed = (input_tokens + gate * velocity).astype(jnp.bfloat16)
     dvel = (output_cotangent.astype(jnp.float32) * gate).astype(jnp.bfloat16)
-    full_dvel = lax.all_gather(dvel, "tensor", axis=1, tiled=True)
+    full_dvel = jnp.concatenate(
+        lax.all_to_all(
+            jnp.stack(lax.axis_size("tensor") * [dvel]),
+            concat_axis=0,
+            axis_name="tensor",
+            split_axis=0,
+        ),
+        axis=1,
+    )
     dact = jnp.dot(full_dvel, down_weight, preferred_element_type=jnp.float32)
     pull = jax.vjp(gelu_tanh, pre)[1]
     dpre = pull(dact)[0].astype(jnp.bfloat16)

time: 723 us -> 690 us (0.954)
  waiting for transfers between devices: 524 us -> 442 us
  blocking collectives: 141 us -> 192 us
    all_gather x1 -> x0, waiting for transfers between devices: 84.3 us -> none  [on_device(): full_dvel = lax.all_gather(dvel, 'tensor', axis=1, tiled=True)]
    all_to_all x0 -> x1, blocking collectives: none -> 51.4 us  [on_device(): lax.all_to_all(jnp.stack(lax.axis_size('tensor') * [dvel]), concat_axis=0...]
    unnamed x15 -> x17, local copies, waits for them, and re-layouts: 15 us -> 16.6 us
    unnamed x8 -> x7, waiting for transfers between devices: 218 us -> 219 us
  transfers between devices with their start and end apart: 6 -> 5, of which waited for: 6 -> 5; matrix products, arithmetic and copies ran while one was open for 2% -> 2% of each run, Pallas kernels for 0% -> 0%
where the time goes in v1:
time: 690 us
  waiting for transfers between devices  442 us (64%)
  blocking collectives  192 us (28%)
  local copies, waits for them, and re-layouts  20.5 us (3%)
  matrix products  18.9 us (3%)
  between operations  13.9 us (2%)
    unnamed x7, waiting for transfers between devices  219 us
    reduce_scatter x1, waiting for transfers between devices, on_device(): lax.psum_scatter(lax.dot_general(cols, dpre, (((0,), (0,)), ((), ())), pr...  107 us
    all_gather x1, waiting for transfers between devices, on_device(): full_in = lax.all_gather(hidden_input_rows, 'tensor', axis=1, tiled=True)  78.6 us
    psum x1, blocking collectives, on_device(): lax.psum((jnp.sum(normalized_input_gradient, axis=1), jnp.sum(normalized_...  71.7 us
    psum x1, blocking collectives, on_device(): lax.psum((jnp.sum(input_tokens, axis=1), jnp.sum(input_tokens * input_tok...  68.9 us
    all_to_all x1, blocking collectives, on_device(): lax.all_to_all(jnp.stack(lax.axis_size('tensor') * [dvel]), concat_axis=0...  51.4 us
    reduce_scatter x1, waiting for transfers between devices, on_device(): lax.psum_scatter(lax.dot_general(cols, act, (((0,), (0,)), ((), ())), pre...  36.6 us
    unnamed x17, local copies, waits for them, and re-layouts  16.6 us
  transfers between devices with their start and end apart: 5, of which 5 were waited for; matrix products, arithmetic and copies ran while one was open for 2% of the time, Pallas kernels for 0%

profile of v1, /device:TPU:1, one launch (start us, length us, event | category | flops | bytes accessed | tf_op | source)
XLA Modules:
  0.0 689.6 jit_solution(454933059821965631)
XLA Ops:
  7.2 0.0 all-gather.2.cloned.1.call-start
  7.2 0.8 compare_and_fusion
  8.1 0.7 compare_select_fusion
  8.8 0.9 copy.21
  9.7 0.1 convert_reduce_fusion
  9.8 2.8 copy.22
  12.6 2.6 gather_fusion
  15.2 0.3 broadcast_select_fusion
  15.5 0.3 fusion.23
  15.8 68.9 %all-reduce.1 = (f32[256]{0:T(256)S(1)}, f32[256]{0:T(256)S(1)}) all-reduce(f32[256]{0:T(256)S(1)} %get-tuple-element.19, f32[256]{0:T(256)S(1)} %get-tuple-element.18), channel_id=1, replica_groups=mesh['dp'=8,'tensor'=32] {'tensor'}, use_global_device_ids=true, to_apply=%region_3.4 | all-reduce | flops 512 | bytes 4096 | tf_op jit(solution)/shard_map/psum | solution.py:19
  84.7 0.1 fusion.14
  84.9 0.7 copy.25
  85.6 0.0 all-gather.2.cloned.1.call-update
  85.6 0.0 reduce-scatter.13.cloned.1.call-start
  85.7 78.6 %all-gather.2.cloned.1.call-done = bf16[256,3072]{0,1:T(8,128)(2,1)} async-done(((bf16[256,96]{0,1:T(8,128)(2,1)}), bf16[256,3072]{0,1:T(8,128)(2,1)}) %all-gather.2.cloned.1.call-update) | async-done | bytes 1572880 | tf_op jit(solution)/shard_map/all_gather | solution.py:29
  164.3 3.2 fusion.24
  167.5 2.7 convolution_bitcast_fusion.1
  170.2 3.5 copy.30
  173.8 0.0 reduce-scatter.13.cloned.1.call-update
  173.8 0.0 reduce-scatter.15.cloned.1.call-start
  173.9 0.7 copy-done.3
  174.6 0.1 copy.26
  174.7 113.5 %reduce-scatter.13.cloned.1.call-done = f32[96,256]{1,0:T(8,128)} async-done(((f32[3072,256]{1,0:T(8,128)}), f32[96,256]{1,0:T(8,128)}) %reduce-scatter.13.cloned.1.call-update) | async-done | bytes 98320
  288.2 1.0 copy.31
  289.2 0.1 copy.27
  289.3 0.2 stack.2
  289.5 51.4 %all_to_all.5 = bf16[32,256,96]{1,2,0:T(8,128)(2,1)S(1)} all-to-all(bf16[32,256,96]{1,2,0:T(8,128)(2,1)S(1)} %stack.2), channel_id=1, replica_groups=mesh['dp'=8,'tensor'=32] {'tensor'}, dimensions={0} | all-to-all | bytes 3145728 | tf_op jit(solution)/shard_map/all_to_all | solution.py:42
  340.9 1.2 copy-done.1
  342.0 1.2 fusion.6
  343.2 0.5 copy-done.2
  343.7 2.7 convolution_bitcast_fusion
  346.4 3.5 copy.32
  349.9 0.0 reduce-scatter.15.cloned.1.call-update
  349.9 0.0 reduce-scatter.11.cloned.1.call-start
  350.0 4.6 fusion.22
  354.6 0.0 reduce-scatter.11.cloned.1.call-update
  354.6 0.0 reduce-scatter.9.cloned.1.call-start
  354.7 4.6 fusion.25
  359.2 0.0 reduce-scatter.9.cloned.1.call-update
  359.3 0.7 copy.28
  360.0 105.9 %reduce-scatter.15.cloned.1.call-done = f32[96,256]{1,0:T(8,128)} async-done(((f32[3072,256]{1,0:T(8,128)}), f32[96,256]{1,0:T(8,128)}) %reduce-scatter.15.cloned.1.call-update) | async-done | bytes 98320
  465.9 1.0 copy.33
  466.9 0.2 fusion.21
  467.1 71.7 %all-reduce = (f32[256]{0:T(256)S(1)}, f32[256]{0:T(256)S(1)}) all-reduce(f32[256]{0:T(256)S(1)} %get-tuple-element.17, f32[256]{0:T(256)S(1)} %get-tuple-element.16), channel_id=1, replica_groups=mesh['dp'=8,'tensor'=32] {'tensor'}, use_global_device_ids=true, to_apply=%region_9.10 | all-reduce | flops 512 | bytes 4096 | tf_op jit(solution)/shard_map/psum | solution.py:61
  538.8 0.2 fusion.8
  539.0 0.7 copy.29
  539.7 36.6 %reduce-scatter.11.cloned.1.call-done = f32[384,384]{1,0:T(8,128)} async-done(((f32[3072,384]{1,0:T(8,128)}), f32[384,384]{1,0:T(8,128)}) %reduce-scatter.11.cloned.1.call-update) | async-done | bytes 589840 | tf_op jit(solution)/shard_map/reduce_scatter | solution.py:81
  576.4 106.7 %reduce-scatter.9.cloned.1.call-done = f32[384,384]{1,0:T(8,128)} async-done(((f32[3072,384]{1,0:T(8,128)}), f32[384,384]{1,0:T(8,128)}) %reduce-scatter.9.cloned.1.call-update) | async-done | bytes 589840 | tf_op jit(solution)/shard_map/reduce_scatter | solution.py:74
  (9 shorter events, 0.1 us)
Async XLA Ops:
  7.2 160.3 %copy-start = (bf16[3072,384]{1,0:T(8,128)(2,1)S(1)}, bf16[3072,384]{1,0:T(8,128)(2,1)}, u32[]{:S(2)}) copy-start(bf16[3072,384]{1,0:T(8,128)(2,1)} %param.10) | copy-start | bytes 7077892
  7.2 157.2 %all-gather.2.cloned.1.call-start = ((), (), s32[]{:S(2)}) async-start(), calls=%async_computation.5 | async-start | bytes 1622016 | tf_op jit(solution)/shard_map/all_gather | solution.py:29
  85.6 202.5 %reduce-scatter.13.cloned.1.call-start = ((), (), s32[]{:S(2)}) async-start(), calls=%async_computation.8 | async-start | bytes 3244032
  173.8 0.8 copy-start.3
  173.8 292.1 %reduce-scatter.15.cloned.1.call-start = ((), (), s32[]{:S(2)}) async-start(), calls=%async_computation.9 | async-start | bytes 3244032
  340.9 1.2 copy-start.1
  342.0 1.7 copy-start.2
  349.9 226.4 %reduce-scatter.11.cloned.1.call-start = ((), (), s32[]{:S(2)}) async-start(), calls=%async_computation.7 | async-start | bytes 5308416 | tf_op jit(solution)/shard_map/reduce_scatter | solution.py:81
  354.6 328.5 %reduce-scatter.9.cloned.1.call-start = ((), (), s32[]{:S(2)}) async-start(), calls=%async_computation.6 | async-start | bytes 5308416 | tf_op jit(solution)/shard_map/reduce_scatter | solution.py:74
Sparse Core Ops, SparseCore 0:
  85.8 78.5 all-gather.1
  173.9 114.2 reduce-scatter.12
  350.1 115.8 reduce-scatter.14
  468.9 107.4 reduce-scatter.10
  579.4 103.7 reduce-scatter.8
